TPU v7x, 32 devices: a whole 2x2x4 slice. The times are simulated.
32 devices in a mesh: seq: 8 (over z, y), pack: 4 (over x, core).
Axes of the slice: x: 2, y: 2, z: 4, core: 2. Of those that a mesh axis runs over, the one named last changes fastest.
Arguments:
- queries: bfloat16 [8192, 2048], P(('pack', 'seq')), parts along dimension 0, may hold values from -10 to 10
- keys: bfloat16 [8192, 512], P(('pack', 'seq')), parts along dimension 0, may hold values from -10 to 10
- values: bfloat16 [8192, 512], P(('pack', 'seq')), parts along dimension 0, may hold values from -6 to 6
- lengths: int32 [32], P('pack'), parts along dimension 0, may hold values from 1 to 1024, 2048 in all
- home: int32 [64], P('pack'), parts along dimension 0, may hold values from 0 to 7, as said below
Outputs:
- attended: bfloat16 [8192, 2048], P(('pack', 'seq')), parts along dimension 0
There are 4 independent parts, one for each index of `pack`. A program takes and returns all parts, laid end to end along the dimension named above; each array names one. Nothing has to cross between parts.
Inputs may be any that keep to these rules, and one draw needn't show every extreme that they name: Block b covers positions b * 128 to b * 128 + 127. home[b] is 2 * (b // 4) or that plus one, and every device index is home of exactly 2 blocks.
All inputs are finite; a program needn't handle non-finite values.
Results may differ from a plain program's by a relative error of at most 0.0033.
Values may be sent and summed in bfloat16 or wider, within the bound.
A program may use at most 64 MiB of HBM per device.

v0:
```python
import functools

import jax
import jax.numpy as jnp
from jax import lax
from jax.experimental import pallas as pl
from jax.experimental.pallas import tpu as pltpu
from jax.sharding import PartitionSpec as P

HD = 128
BLOCK = 128
WINDOW = 2048
LOG2E = 1.4426950408889634
FAR = float(2**20)
MESH = pl.DeviceIdType.MESH


def spans(row_block, depth, blocks, reach):
    found = []
    for back in range(depth, -1, -1):
        near = [
            kb
            for kb in range(blocks)
            if -BLOCK < (back * blocks + row_block - kb) * BLOCK < reach + BLOCK - 1
        ]
        if near:
            found.append((back, near[0], near[-1] + 1))
    return found


def fused(
    plan, lengths, home, queries, keys, values, out,
    q, kv, qext, kext, mixed, give, keep,
    load_sem, q_load, q_send, q_recv, kv_send, kv_recv, hop_send, hop_recv, o_send, o_recv, o_keep,
):
    group, halves, depth, reach, windowed, chunk = plan
    rows = queries.shape[0]
    blocks = 2 * rows // BLOCK
    per = blocks // 2
    me = lax.axis_index("seq")
    count = lax.axis_size("seq")
    other = me ^ 1
    parity = me % 2
    pair = me // 2
    last = count // 2 - 1
    scale = HD ** (-0.5) * LOG2E

    def columns(head, wide=1):
        return pl.ds(pl.multiple_of(head * HD, HD), wide * HD)

    def load_kv(h, t):
        source = keys if t == 0 else values
        return pltpu.make_async_copy(
            source.at[:, columns(parity * halves + h)], kv.at[h, t, 0, parity], load_sem.at[h, t]
        )

    def load_q(h, g):
        return pltpu.make_async_copy(
            queries.at[:, columns((parity * halves + h) * group + g)],
            q.at[h, g, parity],
            q_load.at[h, g],
        )

    def swap_kv(h, t):
        source = keys if t == 0 else values
        return pltpu.make_async_remote_copy(
            source.at[:, columns((1 - parity) * halves + h)],
            kv.at[h, t, 0, parity],
            kv_send.at[h, t],
            kv_recv.at[h, t],
            device_id={"seq": other},
            device_id_type=MESH,
        )

    def swap_q(h, g):
        return pltpu.make_async_remote_copy(
            queries.at[:, columns(((1 - parity) * halves + h) * group + g)],
            q.at[h, g, parity],
            q_send.at[h, g],
            q_recv.at[h, g],
            device_id={"seq": other},
            device_id_type=MESH,
        )

    def hop(h, back, side):
        return pltpu.make_async_remote_copy(
            kv.at[h, :, back, side],
            kv.at[h, :, back + 1, side],
            hop_send.at[h, back, side],
            hop_recv.at[h, back, side],
            device_id={"seq": me + 2},
            device_id_type=MESH,
        )

    def send_out(h, g):
        return pltpu.make_async_remote_copy(
            give.at[h, g],
            out.at[:, columns((parity * halves + h) * group + g)],
            o_send.at[h, g],
            o_recv.at[h, g],
            device_id={"seq": other},
            device_id_type=MESH,
        )

    def keep_out(h, g):
        return pltpu.make_async_copy(
            keep.at[h, g], out.at[:, columns((parity * halves + h) * group + g)], o_keep.at[h, g]
        )

    def forward(h, back, side):
        if back > 0:

            @pl.when(pair >= back)
            def _():
                hop(h, back - 1, side).wait_recv()

        if back < depth:

            @pl.when((pair >= back) & (pair < last))
            def _():
                hop(h, back, side).start()

    for h in range(halves):
        for t in range(2):
            load_kv(h, t).start()
    for h in range(halves):
        for g in range(group):
            load_q(h, g).start()

    barrier = pltpu.get_barrier_semaphore()
    pl.semaphore_signal(barrier, inc=1, device_id={"seq": other}, device_id_type=MESH)

    @pl.when(pair > 0)
    def _():
        pl.semaphore_signal(barrier, inc=1, device_id={"seq": me - 2}, device_id_type=MESH)

    pl.semaphore_wait(barrier, 1 + (pair < last).astype(jnp.int32))

    for h in range(halves):
        for t in range(2):
            swap_kv(h, t).start()
    for h in range(halves):
        for t in range(2):
            load_kv(h, t).wait()
        forward(h, 0, parity)
    for h in range(halves):
        for g in range(group):
            swap_q(h, g).start()

    docs = lengths.shape[0]
    lane = lax.broadcasted_iota(jnp.int32, (8, HD), 1)

    def add_doc(doc, state):
        begin, starts, ends = state
        end = begin + lengths[doc]
        here = lane == doc
        return end, jnp.where(here, begin, starts), jnp.where(here, end, ends)

    nothing = jnp.zeros((8, HD), jnp.int32)
    _, starts, ends = lax.fori_loop(
        0, docs, add_doc, (jnp.int32(0), nothing, nothing), unroll=docs <= 16
    )
    starts, ends = starts[:1], ends[:1]
    offset = lax.broadcasted_iota(jnp.int32, (2 * rows, HD), 0)
    for back in range(depth + 1):
        position = (pair - back) * 2 * rows + offset
        inside = ((position >= starts) & (position < ends)) | (position < 0)
        kext[back] = jnp.where(inside, 1.0, 0.0).astype(kext.dtype)
        if back == 0:
            qext[...] = jnp.where(inside, 0.0, -FAR).astype(qext.dtype)
        else:

            @pl.when(pair < back)
            def _():
                for h in range(halves):
                    kv[h, :, back] = jnp.zeros(kv.shape[1:2] + kv.shape[3:], kv.dtype)

    mine = [(home[pair * blocks + b] == me).astype(jnp.int32) for b in range(blocks)]
    kept_at = [jnp.int32(0)] * per
    sent_at = [jnp.int32(0)] * per
    kept_count, sent_count = jnp.int32(0), jnp.int32(0)
    for b in range(blocks):
        for s in range(per):
            kept_at[s] = jnp.where((mine[b] == 1) & (kept_count == s), b, kept_at[s])
            sent_at[s] = jnp.where((mine[b] == 0) & (sent_count == s), b, sent_at[s])
        kept_count = kept_count + mine[b]
        sent_count = sent_count + 1 - mine[b]

    def take_swapped(h):
        for t in range(2):
            swap_kv(h, t).wait_recv()
        forward(h, 0, 1 - parity)

    def keys_of(h, t, back, low, high):
        joined = kv[h, t, back].reshape(2 * rows, HD)
        return joined[low * BLOCK : high * BLOCK]

    def attend(h, first):
        for j in range(blocks):
            side, inner = j // per, j % per
            runs = spans(j, depth, blocks, reach)
            at = pl.ds(inner * BLOCK, BLOCK)
            block = jnp.concatenate([q[h, first + g, side, at] for g in range(chunk)], axis=0)
            extra = jnp.concatenate([qext[pl.ds(j * BLOCK, BLOCK)]] * chunk, axis=0)
            grouped = jnp.concatenate([block, extra], axis=1)
            seen = jnp.concatenate(
                [
                    jnp.concatenate(
                        [keys_of(h, 0, back, low, high), kext[back, low * BLOCK : high * BLOCK]],
                        axis=1,
                    )
                    for back, low, high in runs
                ],
                axis=0,
            )
            raw = lax.dot_general(
                grouped, seen, (((1,), (1,)), ((), ())), preferred_element_type=jnp.float32
            )
            parts = []
            begin = 0
            for back, low, high in runs:
                for kb in range(low, high):
                    part = raw[:, begin : begin + BLOCK]
                    begin += BLOCK
                    gap = (back * blocks + j - kb) * BLOCK
                    row = lax.broadcasted_iota(jnp.int32, (BLOCK, BLOCK), 0)
                    column = lax.broadcasted_iota(jnp.int32, (BLOCK, BLOCK), 1)
                    allowed = None
                    if gap < BLOCK:
                        allowed = gap + row >= column
                    if windowed and gap + BLOCK > WINDOW:
                        allowed = gap + row - column < WINDOW
                    if allowed is not None:
                        shaped = part.reshape(chunk, BLOCK, BLOCK)
                        part = jnp.where(allowed[None], shaped, -FAR).reshape(part.shape)
                    parts.append(part)
            peak = parts[0]
            for part in parts[1:]:
                peak = jnp.maximum(peak, part)
            peak = jnp.max(peak, axis=1, keepdims=True)
            weights = jnp.concatenate(
                [jnp.exp2((part - peak) * scale).astype(jnp.bfloat16) for part in parts], axis=1
            )
            joined = jnp.concatenate(
                [keys_of(h, 1, back, low, high) for back, low, high in runs], axis=0
            )
            joined = jnp.concatenate([joined, jnp.ones_like(joined)], axis=1)
            both = jnp.dot(weights, joined, preferred_element_type=jnp.float32)
            result = (both[:, :HD] / both[:, HD:]).astype(mixed.dtype)
            for g in range(chunk):
                mixed[h, first + g, j] = result[g * BLOCK : (g + 1) * BLOCK]

    def deliver(h, first):
        for g in range(chunk):
            for s in range(per):
                give[h, first + g, pl.ds(s * BLOCK, BLOCK)] = mixed[h, first + g, sent_at[s]]
                keep[h, first + g, pl.ds(s * BLOCK, BLOCK)] = mixed[h, first + g, kept_at[s]]
            send_out(h, first + g).start()
            keep_out(h, first + g).start()

    def settle(h):
        for g in range(group):
            load_q(h, g).wait()
            swap_q(h, g).wait_recv()

    for h in range(halves):
        take_swapped(h)
        if h == 0:
            for back in range(1, depth + 1):
                forward(h, back, parity)
                forward(h, back, 1 - parity)
    for h in range(halves):
        settle(h)
        if h > 0:
            for back in range(1, depth + 1):
                forward(h, back, parity)
                forward(h, back, 1 - parity)

        @pl.loop(0, group // chunk)
        def _(step):
            attend(h, step * chunk)
            deliver(h, step * chunk)

    for h in range(halves):
        for t in range(2):
            swap_kv(h, t).wait_send()
        for back in range(depth):
            for side in range(2):

                @pl.when((pair >= back) & (pair < last))
                def _():
                    hop(h, back, side).wait_send()

        for g in range(group):
            swap_q(h, g).wait_send()
            keep_out(h, g).wait()
            send_out(h, g).wait()


def local(queries, keys, values, lengths, home):
    rows, query_cols = queries.shape
    kv_heads = keys.shape[1] // HD
    group = query_cols // HD // kv_heads
    halves = kv_heads // 2
    blocks = 2 * rows // BLOCK
    seq = lax.axis_size("seq")
    tokens = seq * rows
    most_len = min(tokens // 2, 4096)
    reach = min(WINDOW, most_len)
    depth = min(-(-(reach - 1) // (2 * rows)), seq // 2 - 1)
    plan = (group, halves, depth, reach, most_len > WINDOW, 2)
    bf16 = jnp.bfloat16
    dma = pltpu.SemaphoreType.DMA
    anywhere = pl.BlockSpec(memory_space=pl.ANY)
    smem = pl.BlockSpec(memory_space=pltpu.SMEM)
    return pl.pallas_call(
        functools.partial(fused, plan),
        out_shape=jax.ShapeDtypeStruct(queries.shape, bf16),
        in_specs=[smem, smem, anywhere, anywhere, anywhere],
        out_specs=anywhere,
        scratch_shapes=[
            pltpu.VMEM((halves, group, 2, rows, HD), bf16),
            pltpu.VMEM((halves, 2, depth + 1, 2, rows, HD), bf16),
            pltpu.VMEM((2 * rows, HD), bf16),
            pltpu.VMEM((depth + 1, 2 * rows, HD), bf16),
            pltpu.VMEM((halves, group, blocks, BLOCK, HD), bf16),
            pltpu.VMEM((halves, group, rows, HD), bf16),
            pltpu.VMEM((halves, group, rows, HD), bf16),
            dma((halves, 2)),
            dma((halves, group)),
            dma((halves, group)),
            dma((halves, group)),
            dma((halves, 2)),
            dma((halves, 2)),
            dma((halves, depth, 2)),
            dma((halves, depth, 2)),
            dma((halves, group)),
            dma((halves, group)),
            dma((halves, group)),
        ],
        compiler_params=pltpu.CompilerParams(
            collective_id=0, has_side_effects=True, vmem_limit_bytes=48 * 1024 * 1024
        ),
    )(lengths, home, queries, keys, values)


def solution(mesh):
    placed = (
        P(("pack", "seq"), None),
        P(("pack", "seq"), None),
        P(("pack", "seq"), None),
        P("pack"),
        P("pack"),
    )
    return jax.shard_map(
        local, mesh=mesh, in_specs=placed, out_specs=P(("pack", "seq"), None), check_vma=False
    )
```

profile of v0, /device:TPU:24, one launch (start us, length us, event | category | flops | bytes accessed | tf_op | source)
XLA Modules:
  0.0 42.3 jit_solution(12708681978289885877)
XLA Ops:
  0.0 0.0 copy-start
  0.0 1.2 %copy-done = bf16[256,2048]{1,0:T(8,128)(2,1)S(1)} copy-done((bf16[256,2048]{1,0:T(8,128)(2,1)S(1)}, bf16[256,2048]{1,0:T(8,128)(2,1)}, u32[]{:S(2)}) %copy-start) | copy-done | bytes 1048600
  1.2 0.0 copy-start.1
  1.2 0.9 %copy-done.1 = bf16[256,512]{1,0:T(8,128)(2,1)S(1)} copy-done((bf16[256,512]{1,0:T(8,128)(2,1)S(1)}, bf16[256,512]{1,0:T(8,128)(2,1)}, u32[]{:S(2)}) %copy-start.1) | copy-done | bytes 262168
  2.2 0.0 copy-start.2
  2.2 0.9 %copy-done.2 = bf16[256,512]{1,0:T(8,128)(2,1)S(1)} copy-done((bf16[256,512]{1,0:T(8,128)(2,1)S(1)}, bf16[256,512]{1,0:T(8,128)(2,1)}, u32[]{:S(2)}) %copy-start.2) | copy-done | bytes 262168
  3.1 0.0 copy-start.3
  3.1 0.7 %copy-done.3 = s32[8]{0:T(128)S(1)} copy-done((s32[8]{0:T(128)S(1)}, s32[8]{0:T(128)}, u32[]{:S(2)}) %copy-start.3) | copy-done | bytes 56
  3.8 0.0 copy-start.4
  3.8 0.7 %copy-done.4 = s32[16]{0:T(128)S(1)} copy-done((s32[16]{0:T(128)S(1)}, s32[16]{0:T(128)}, u32[]{:S(2)}) %copy-start.4) | copy-done | bytes 88
  4.4 36.9 %shard_map.55 = bf16[256,2048]{1,0:T(8,128)(2,1)S(1)} custom-call(s32[8]{0:T(128)S(1)} %copy-done.3, s32[16]{0:T(128)S(1)} %copy-done.4, bf16[256,2048]{1,0:T(8,128)(2,1)S(1)} %copy-done, bf16[256,512]{1,0:T(8,128)(2,1)S(1)} %copy-done.1, bf16[256,512]{1,0:T(8,128)(2,1)S(1)} %copy-done.2), custom_call_target="tpu_custom_call" | custom-call | tf_op jit(solution)/shard_map/pallas_call | solution.py:316
  41.3 1.0 %copy.7 = bf16[256,2048]{1,0:T(8,128)(2,1)} copy(bf16[256,2048]{1,0:T(8,128)(2,1)S(1)} %shard_map.55) | data formatting | bytes 2097152
Async XLA Ops:
  0.0 1.2 %copy-start = (bf16[256,2048]{1,0:T(8,128)(2,1)S(1)}, bf16[256,2048]{1,0:T(8,128)(2,1)}, u32[]{:S(2)}) copy-start(bf16[256,2048]{1,0:T(8,128)(2,1)} %queries.1) | copy-start | bytes 3145732
  1.2 0.9 %copy-start.1 = (bf16[256,512]{1,0:T(8,128)(2,1)S(1)}, bf16[256,512]{1,0:T(8,128)(2,1)}, u32[]{:S(2)}) copy-start(bf16[256,512]{1,0:T(8,128)(2,1)} %keys.1) | copy-start | bytes 786436
  2.2 0.9 %copy-start.2 = (bf16[256,512]{1,0:T(8,128)(2,1)S(1)}, bf16[256,512]{1,0:T(8,128)(2,1)}, u32[]{:S(2)}) copy-start(bf16[256,512]{1,0:T(8,128)(2,1)} %values.1) | copy-start | bytes 786436
  3.1 0.7 %copy-start.3 = (s32[8]{0:T(128)S(1)}, s32[8]{0:T(128)}, u32[]{:S(2)}) copy-start(s32[8]{0:T(128)} %lengths.1) | copy-start | bytes 100
  3.8 0.7 %copy-start.4 = (s32[16]{0:T(128)S(1)}, s32[16]{0:T(128)}, u32[]{:S(2)}) copy-start(s32[16]{0:T(128)} %home.1) | copy-start | bytes 196
where the time goes:
time: 42.5 us; the launch traced here: 42.3 us
  Pallas kernels  36.9 us (87%)
  local copies, waits for them, and re-layouts  5.41 us (13%)
    pallas_call x1, Pallas kernels, local(): pl.pallas_call(functools.partial(fused, plan), out_shape=jax.ShapeDtypeSt...  36.9 us
    unnamed x11, local copies, waits for them, and re-layouts  5.41 us

commit v1 on v0

--- a/solution.py
+++ b/solution.py
@@ -29,9 +29,9 @@
 
 
 def fused(
-    plan, lengths, home, queries, keys, values, out,
-    q, kv, qext, kext, mixed, give, keep,
-    load_sem, q_load, q_send, q_recv, kv_send, kv_recv, hop_send, hop_recv, o_send, o_recv, o_keep,
+    plan, lengths_in, home_in, queries, keys, values, out,
+    lengths, home, q, kv, qext, kext, mixed, give, keep,
+    small_sem, load_sem, q_load, q_send, q_recv, kv_send, kv_recv, hop_send, hop_recv, o_send, o_recv, o_keep,
 ):
     group, halves, depth, reach, windowed, chunk = plan
     rows = queries.shape[0]
@@ -120,9 +120,15 @@
             def _():
                 hop(h, back, side).start()
 
+    small = [
+        pltpu.make_async_copy(lengths_in, lengths, small_sem.at[0]),
+        pltpu.make_async_copy(home_in, home, small_sem.at[1]),
+    ]
     for h in range(halves):
         for t in range(2):
             load_kv(h, t).start()
+    for copy in small:
+        copy.start()
     for h in range(halves):
         for g in range(group):
             load_q(h, g).start()
@@ -146,6 +152,9 @@
     for h in range(halves):
         for g in range(group):
             swap_q(h, g).start()
+
+    for copy in small:
+        copy.wait()
 
     docs = lengths.shape[0]
     lane = lax.broadcasted_iota(jnp.int32, (8, HD), 1)
@@ -312,13 +321,15 @@
     bf16 = jnp.bfloat16
     dma = pltpu.SemaphoreType.DMA
     anywhere = pl.BlockSpec(memory_space=pl.ANY)
-    smem = pl.BlockSpec(memory_space=pltpu.SMEM)
+    hbm = pl.BlockSpec(memory_space=pltpu.HBM)
     return pl.pallas_call(
         functools.partial(fused, plan),
-        out_shape=jax.ShapeDtypeStruct(queries.shape, bf16),
-        in_specs=[smem, smem, anywhere, anywhere, anywhere],
-        out_specs=anywhere,
+        out_shape=pltpu.VMEM(queries.shape, bf16),
+        in_specs=[hbm] * 5,
+        out_specs=pl.BlockSpec(memory_space=pltpu.VMEM),
         scratch_shapes=[
+            pltpu.SMEM(lengths.shape, jnp.int32),
+            pltpu.SMEM(home.shape, jnp.int32),
             pltpu.VMEM((halves, group, 2, rows, HD), bf16),
             pltpu.VMEM((halves, 2, depth + 1, 2, rows, HD), bf16),
             pltpu.VMEM((2 * rows, HD), bf16),
@@ -326,6 +337,7 @@
             pltpu.VMEM((halves, group, blocks, BLOCK, HD), bf16),
             pltpu.VMEM((halves, group, rows, HD), bf16),
             pltpu.VMEM((halves, group, rows, HD), bf16),
+            dma((2,)),
             dma((halves, 2)),
             dma((halves, group)),
             dma((halves, group)),
@@ -339,7 +351,7 @@
             dma((halves, group)),
         ],
         compiler_params=pltpu.CompilerParams(
-            collective_id=0, has_side_effects=True, vmem_limit_bytes=48 * 1024 * 1024
+            collective_id=0, has_side_effects=True, vmem_limit_bytes=60 * 1024 * 1024
         ),
     )(lengths, home, queries, keys, values)
 

time: 42.5 us -> 37.3 us (0.88)
  local copies, waits for them, and re-layouts: 5.41 us -> 0.97 us
  Pallas kernels: 36.9 us -> 36.1 us
    unnamed x11 -> x1, local copies, waits for them, and re-layouts: 5.41 us -> 0.97 us
    pallas_call x1, Pallas kernels: 36.9 us -> 36.1 us  [local(): pl.pallas_call(functools.partial(fused, plan), out_shape=pltpu.VMEM(queri...]
where the time goes in v1:
time: 37.3 us; the launch traced here: 37.1 us
  Pallas kernels  36.1 us (97%)
  local copies, waits for them, and re-layouts  0.97 us (3%)
    pallas_call x1, Pallas kernels, local(): pl.pallas_call(functools.partial(fused, plan), out_shape=pltpu.VMEM(queri...  36.1 us
    unnamed x1, local copies, waits for them, and re-layouts  0.97 us

profile of v1, /device:TPU:24, one launch (start us, length us, event | category | flops | bytes accessed | tf_op | source)
XLA Modules:
  0.0 37.1 jit_solution(8332409995915631745)
XLA Ops:
  0.0 36.1 %shard_map.55 = bf16[256,2048]{1,0:T(8,128)(2,1)S(1)} custom-call(s32[8]{0:T(128)} %lengths_in.1, s32[16]{0:T(128)} %home_in.1, bf16[256,2048]{1,0:T(8,128)(2,1)} %queries.1, bf16[256,512]{1,0:T(8,128)(2,1)} %keys.1, bf16[256,512]{1,0:T(8,128)(2,1)} %values.1), custom_call_target="tpu_custom_call" | custom-call | tf_op jit(solution)/shard_map/pallas_call | solution.py:325
  36.2 1.0 %copy.7 = bf16[256,2048]{1,0:T(8,128)(2,1)} copy(bf16[256,2048]{1,0:T(8,128)(2,1)S(1)} %shard_map.55) | data formatting | bytes 2097152

commit v2 on v1

--- a/solution.py
+++ b/solution.py
@@ -30,7 +30,7 @@
 
 def fused(
     plan, lengths_in, home_in, queries, keys, values, out,
-    lengths, home, q, kv, qext, kext, mixed, give, keep,
+    lengths, home, q, kv, qext, kext, mixed, give, keep, top, part_sum,
     small_sem, load_sem, q_load, q_send, q_recv, kv_send, kv_recv, hop_send, hop_recv, o_send, o_recv, o_keep,
 ):
     group, halves, depth, reach, windowed, chunk = plan
@@ -201,63 +201,107 @@
         forward(h, 0, 1 - parity)
 
     def keys_of(h, t, back, low, high):
-        joined = kv[h, t, back].reshape(2 * rows, HD)
-        return joined[low * BLOCK : high * BLOCK]
-
-    def attend(h, first):
+        found = []
+        for side in range(2):
+            begin, end = max(low - side * per, 0), min(high - side * per, per)
+            if begin < end:
+                at = pl.ds(begin * BLOCK, (end - begin) * BLOCK)
+                found.append(kv[h, t, back, side, at])
+        return jnp.concatenate(found, axis=0)
+
+    def split(j, late):
+        early, rest = [], []
+        for back, low, high in spans(j, depth, blocks, reach):
+            if late is None or back < depth:
+                early.append((back, low, high))
+                continue
+            begin, end = max(low, late * per), min(high, (late + 1) * per)
+            if begin < end:
+                rest.append((back, begin, end))
+            for begin, end in ((low, min(high, late * per)), (max(low, (late + 1) * per), high)):
+                if begin < end:
+                    early.append((back, begin, end))
+        return early, rest
+
+    def scored(h, first, j, runs):
+        side, inner = j // per, j % per
+        at = pl.ds(inner * BLOCK, BLOCK)
+        block = jnp.concatenate([q[h, first + g, side, at] for g in range(chunk)], axis=0)
+        extra = jnp.concatenate([qext[pl.ds(j * BLOCK, BLOCK)]] * chunk, axis=0)
+        grouped = jnp.concatenate([block, extra], axis=1)
+        seen = jnp.concatenate(
+            [
+                jnp.concatenate(
+                    [keys_of(h, 0, back, low, high), kext[back, low * BLOCK : high * BLOCK]],
+                    axis=1,
+                )
+                for back, low, high in runs
+            ],
+            axis=0,
+        )
+        raw = lax.dot_general(
+            grouped, seen, (((1,), (1,)), ((), ())), preferred_element_type=jnp.float32
+        )
+        parts = []
+        begin = 0
+        for back, low, high in runs:
+            for kb in range(low, high):
+                part = raw[:, begin : begin + BLOCK]
+                begin += BLOCK
+                gap = (back * blocks + j - kb) * BLOCK
+                row = lax.broadcasted_iota(jnp.int32, (BLOCK, BLOCK), 0)
+                column = lax.broadcasted_iota(jnp.int32, (BLOCK, BLOCK), 1)
+                allowed = None
+                if gap < BLOCK:
+                    allowed = gap + row >= column
+                if windowed and gap + BLOCK > WINDOW:
+                    allowed = gap + row - column < WINDOW
+                if allowed is not None:
+                    shaped = part.reshape(chunk, BLOCK, BLOCK)
+                    part = jnp.where(allowed[None], shaped, -FAR).reshape(part.shape)
+                parts.append(part)
+        peak = parts[0]
+        for part in parts[1:]:
+            peak = jnp.maximum(peak, part)
+        return parts, jnp.max(peak, axis=1, keepdims=True)
+
+    def folded(h, parts, peak, runs):
+        weights = jnp.concatenate(
+            [jnp.exp2((part - peak) * scale).astype(jnp.bfloat16) for part in parts], axis=1
+        )
+        joined = jnp.concatenate(
+            [keys_of(h, 1, back, low, high) for back, low, high in runs], axis=0
+        )
+        joined = jnp.concatenate([joined, jnp.ones_like(joined)], axis=1)
+        return jnp.dot(weights, joined, preferred_element_type=jnp.float32)
+
+    def finish(h, first, j, both):
+        result = (both[:, :HD] / both[:, HD:]).astype(mixed.dtype)
+        for g in range(chunk):
+            mixed[h, first + g, j] = result[g * BLOCK : (g + 1) * BLOCK]
+
+    def attend(h, step, late=None):
         for j in range(blocks):
-            side, inner = j // per, j % per
-            runs = spans(j, depth, blocks, reach)
-            at = pl.ds(inner * BLOCK, BLOCK)
-            block = jnp.concatenate([q[h, first + g, side, at] for g in range(chunk)], axis=0)
-            extra = jnp.concatenate([qext[pl.ds(j * BLOCK, BLOCK)]] * chunk, axis=0)
-            grouped = jnp.concatenate([block, extra], axis=1)
-            seen = jnp.concatenate(
-                [
-                    jnp.concatenate(
-                        [keys_of(h, 0, back, low, high), kext[back, low * BLOCK : high * BLOCK]],
-                        axis=1,
-                    )
-                    for back, low, high in runs
-                ],
-                axis=0,
-            )
-            raw = lax.dot_general(
-                grouped, seen, (((1,), (1,)), ((), ())), preferred_element_type=jnp.float32
-            )
-            parts = []
-            begin = 0
-            for back, low, high in runs:
-                for kb in range(low, high):
-                    part = raw[:, begin : begin + BLOCK]
-                    begin += BLOCK
-                    gap = (back * blocks + j - kb) * BLOCK
-                    row = lax.broadcasted_iota(jnp.int32, (BLOCK, BLOCK), 0)
-                    column = lax.broadcasted_iota(jnp.int32, (BLOCK, BLOCK), 1)
-                    allowed = None
-                    if gap < BLOCK:
-                        allowed = gap + row >= column
-                    if windowed and gap + BLOCK > WINDOW:
-                        allowed = gap + row - column < WINDOW
-                    if allowed is not None:
-                        shaped = part.reshape(chunk, BLOCK, BLOCK)
-                        part = jnp.where(allowed[None], shaped, -FAR).reshape(part.shape)
-                    parts.append(part)
-            peak = parts[0]
-            for part in parts[1:]:
-                peak = jnp.maximum(peak, part)
-            peak = jnp.max(peak, axis=1, keepdims=True)
-            weights = jnp.concatenate(
-                [jnp.exp2((part - peak) * scale).astype(jnp.bfloat16) for part in parts], axis=1
-            )
-            joined = jnp.concatenate(
-                [keys_of(h, 1, back, low, high) for back, low, high in runs], axis=0
-            )
-            joined = jnp.concatenate([joined, jnp.ones_like(joined)], axis=1)
-            both = jnp.dot(weights, joined, preferred_element_type=jnp.float32)
-            result = (both[:, :HD] / both[:, HD:]).astype(mixed.dtype)
-            for g in range(chunk):
-                mixed[h, first + g, j] = result[g * BLOCK : (g + 1) * BLOCK]
+            early, rest = split(j, late)
+            parts, peak = scored(h, step * chunk, j, early)
+            both = folded(h, parts, peak, early)
+            if rest:
+                top[step, j] = jnp.broadcast_to(peak, top.shape[2:])
+                part_sum[step, j] = both
+            else:
+                finish(h, step * chunk, j, both)
+
+    def complete(h, step, late):
+        for j in range(blocks):
+            _, rest = split(j, late)
+            if rest:
+                parts, peak = scored(h, step * chunk, j, rest)
+                before = top[step, j]
+                peak = jnp.maximum(before, peak)
+                rescale = jnp.exp2((before - peak) * scale)
+                both = folded(h, parts, peak, rest)
+                both = both + part_sum[step, j] * jnp.concatenate([rescale, rescale], axis=1)
+                finish(h, step * chunk, j, both)
 
     def deliver(h, first):
         for g in range(chunk):
@@ -272,22 +316,51 @@
             load_q(h, g).wait()
             swap_q(h, g).wait_recv()
 
-    for h in range(halves):
+    def arrive(h, backs, sides):
+        for back in backs:
+            for side in sides:
+                forward(h, back, side)
+
+    sides = (parity, 1 - parity)
+    steps = group // chunk
+    soon = range(1, 2 if depth > 1 else 1)
+    take_swapped(0)
+    arrive(0, soon, sides)
+    for h in range(1, halves):
         take_swapped(h)
-        if h == 0:
-            for back in range(1, depth + 1):
-                forward(h, back, parity)
-                forward(h, back, 1 - parity)
+        arrive(h, soon, sides[:1])
     for h in range(halves):
         settle(h)
-        if h > 0:
-            for back in range(1, depth + 1):
-                forward(h, back, parity)
-                forward(h, back, 1 - parity)
-
-        @pl.loop(0, group // chunk)
+        later = range(soon.stop, depth + 1)
+        if h + 1 < halves or depth == 0:
+            arrive(h, later, sides)
+            for step in range(steps):
+                attend(h, step)
+                deliver(h, step * chunk)
+                if step == 0 and h + 1 < halves:
+                    arrive(h + 1, soon, sides[1:])
+            continue
+        arrive(h, later[:-1], sides)
+        arrive(h, later[-1:], sides[:1])
+
+        @pl.loop(0, steps)
         def _(step):
-            attend(h, step * chunk)
+            for side in range(2):
+
+                @pl.when(parity == side)
+                def _():
+                    attend(h, step, 1 - side)
+
+        arrive(h, later[-1:], sides[1:])
+
+        @pl.loop(0, steps)
+        def _(step):
+            for side in range(2):
+
+                @pl.when(parity == side)
+                def _():
+                    complete(h, step, 1 - side)
+
             deliver(h, step * chunk)
 
     for h in range(halves):
@@ -337,6 +410,8 @@
             pltpu.VMEM((halves, group, blocks, BLOCK, HD), bf16),
             pltpu.VMEM((halves, group, rows, HD), bf16),
             pltpu.VMEM((halves, group, rows, HD), bf16),
+            pltpu.VMEM((group // plan[-1], blocks, plan[-1] * BLOCK, HD), jnp.float32),
+            pltpu.VMEM((group // plan[-1], blocks, plan[-1] * BLOCK, 2 * HD), jnp.float32),
             dma((2,)),
             dma((halves, 2)),
             dma((halves, group)),

time: 37.3 us -> 35.7 us (0.957)
  Pallas kernels: 36.1 us -> 34.6 us
    pallas_call x1, Pallas kernels: 36.1 us -> 34.6 us  [local(): pl.pallas_call(functools.partial(fused, plan), out_shape=pltpu.VMEM(queri...]
where the time goes in v2:
time: 35.7 us; the launch traced here: 35.6 us
  Pallas kernels  34.6 us (97%)
  local copies, waits for them, and re-layouts  0.97 us (3%)
    pallas_call x1, Pallas kernels, local(): pl.pallas_call(functools.partial(fused, plan), out_shape=pltpu.VMEM(queri...  34.6 us
    unnamed x1, local copies, waits for them, and re-layouts  0.97 us

profile of v2, /device:TPU:24, one launch (start us, length us, event | category | flops | bytes accessed | tf_op | source)
XLA Modules:
  0.0 35.6 jit_solution(10178318261522669360)
XLA Ops:
  0.0 34.6 %shard_map.55 = bf16[256,2048]{1,0:T(8,128)(2,1)S(1)} custom-call(s32[8]{0:T(128)} %lengths_in.1, s32[16]{0:T(128)} %home_in.1, bf16[256,2048]{1,0:T(8,128)(2,1)} %queries.1, bf16[256,512]{1,0:T(8,128)(2,1)} %keys.1, bf16[256,512]{1,0:T(8,128)(2,1)} %values.1), custom_call_target="tpu_custom_call" | custom-call | tf_op jit(solution)/shard_map/pallas_call | solution.py:398
  34.6 1.0 %copy.7 = bf16[256,2048]{1,0:T(8,128)(2,1)} copy(bf16[256,2048]{1,0:T(8,128)(2,1)S(1)} %shard_map.55) | data formatting | bytes 2097152

commit v3 on v2

--- a/solution.py
+++ b/solution.py
@@ -209,19 +209,17 @@
                 found.append(kv[h, t, back, side, at])
         return jnp.concatenate(found, axis=0)
 
-    def split(j, late):
-        early, rest = [], []
+    def stages(j, own):
+        found = [[], [], []]
         for back, low, high in spans(j, depth, blocks, reach):
-            if late is None or back < depth:
-                early.append((back, low, high))
+            if back < depth or depth == 0:
+                found[0].append((back, low, high))
                 continue
-            begin, end = max(low, late * per), min(high, (late + 1) * per)
-            if begin < end:
-                rest.append((back, begin, end))
-            for begin, end in ((low, min(high, late * per)), (max(low, (late + 1) * per), high)):
+            for stage, side in ((1, own), (2, 1 - own)):
+                begin, end = max(low, side * per), min(high, (side + 1) * per)
                 if begin < end:
-                    early.append((back, begin, end))
-        return early, rest
+                    found[stage].append((back, begin, end))
+        return found
 
     def scored(h, first, j, runs):
         side, inner = j // per, j % per
@@ -280,28 +278,32 @@
         for g in range(chunk):
             mixed[h, first + g, j] = result[g * BLOCK : (g + 1) * BLOCK]
 
-    def attend(h, step, late=None):
+    def attend(h, step, own, begin, end):
         for j in range(blocks):
-            early, rest = split(j, late)
-            parts, peak = scored(h, step * chunk, j, early)
-            both = folded(h, parts, peak, early)
-            if rest:
+            found = stages(j, own)
+            runs = sum(found[begin:end], [])
+            if not runs:
+                continue
+            parts, peak = scored(h, step * chunk, j, runs)
+            if begin > 0:
+                before = top[step, j]
+                peak = jnp.maximum(before, peak)
+                rescale = jnp.exp2((before - peak) * scale)
+            both = folded(h, parts, peak, runs)
+            if begin > 0:
+                both = both + part_sum[step, j] * jnp.concatenate([rescale, rescale], axis=1)
+            if any(found[end:]):
                 top[step, j] = jnp.broadcast_to(peak, top.shape[2:])
                 part_sum[step, j] = both
             else:
                 finish(h, step * chunk, j, both)
 
-    def complete(h, step, late):
-        for j in range(blocks):
-            _, rest = split(j, late)
-            if rest:
-                parts, peak = scored(h, step * chunk, j, rest)
-                before = top[step, j]
-                peak = jnp.maximum(before, peak)
-                rescale = jnp.exp2((before - peak) * scale)
-                both = folded(h, parts, peak, rest)
-                both = both + part_sum[step, j] * jnp.concatenate([rescale, rescale], axis=1)
-                finish(h, step * chunk, j, both)
+    def by_parity(h, step, begin, end):
+        for side in range(2):
+
+            @pl.when(parity == side)
+            def _():
+                attend(h, step, side, begin, end)
 
     def deliver(h, first):
         for g in range(chunk):
@@ -311,10 +313,10 @@
             send_out(h, first + g).start()
             keep_out(h, first + g).start()
 
-    def settle(h):
-        for g in range(group):
-            load_q(h, g).wait()
-            swap_q(h, g).wait_recv()
+    def settle(h, step):
+        for g in range(chunk):
+            load_q(h, step * chunk + g).wait()
+            swap_q(h, step * chunk + g).wait_recv()
 
     def arrive(h, backs, sides):
         for back in backs:
@@ -329,38 +331,35 @@
     for h in range(1, halves):
         take_swapped(h)
         arrive(h, soon, sides[:1])
-    for h in range(halves):
-        settle(h)
-        later = range(soon.stop, depth + 1)
-        if h + 1 < halves or depth == 0:
-            arrive(h, later, sides)
-            for step in range(steps):
-                attend(h, step)
-                deliver(h, step * chunk)
-                if step == 0 and h + 1 < halves:
-                    arrive(h + 1, soon, sides[1:])
-            continue
+    later = range(soon.stop, depth + 1)
+    for h in range(halves):
+        if h > 0:
+            arrive(h, soon, sides[1:])
         arrive(h, later[:-1], sides)
-        arrive(h, later[-1:], sides[:1])
+        joined = 2 if h == 0 else 1
+        if joined == 2:
+            arrive(h, later[-1:], sides[:1])
 
         @pl.loop(0, steps)
         def _(step):
-            for side in range(2):
-
-                @pl.when(parity == side)
-                def _():
-                    attend(h, step, 1 - side)
+            settle(h, step)
+            if joined == 2:
+                by_parity(h, step, 0, 2)
+            else:
+                attend(h, step, 0, 0, 1)
+
+        if joined == 1:
+            arrive(h, later[-1:], sides[:1])
+
+            @pl.loop(0, steps)
+            def _(step):
+                by_parity(h, step, 1, 2)
 
         arrive(h, later[-1:], sides[1:])
 
         @pl.loop(0, steps)
         def _(step):
-            for side in range(2):
-
-                @pl.when(parity == side)
-                def _():
-                    complete(h, step, 1 - side)
-
+            by_parity(h, step, 2, 3)
             deliver(h, step * chunk)
 
     for h in range(halves):

time: 35.7 us -> 35.1 us (0.983)
  the two profiles are of different devices: /device:TPU:24 before, /device:TPU:0 now
where the time goes in v3:
time: 35.1 us; the launch traced here: 35 us
  Pallas kernels  34 us (97%)
  local copies, waits for them, and re-layouts  0.97 us (3%)
    pallas_call x1, Pallas kernels, local(): pl.pallas_call(functools.partial(fused, plan), out_shape=pltpu.VMEM(queri...  34 us
    unnamed x1, local copies, waits for them, and re-layouts  0.97 us

profile of v3, /device:TPU:0, one launch (start us, length us, event | category | flops | bytes accessed | tf_op | source)
XLA Modules:
  0.0 35.0 jit_solution(9249309921879313457)
XLA Ops:
  0.0 34.0 %shard_map.55 = bf16[256,2048]{1,0:T(8,128)(2,1)S(1)} custom-call(s32[8]{0:T(128)} %lengths_in.1, s32[16]{0:T(128)} %home_in.1, bf16[256,2048]{1,0:T(8,128)(2,1)} %queries.1, bf16[256,512]{1,0:T(8,128)(2,1)} %keys.1, bf16[256,512]{1,0:T(8,128)(2,1)} %values.1), custom_call_target="tpu_custom_call" | custom-call | tf_op jit(solution)/shard_map/pallas_call | solution.py:397
  34.0 1.0 %copy.7 = bf16[256,2048]{1,0:T(8,128)(2,1)} copy(bf16[256,2048]{1,0:T(8,128)(2,1)S(1)} %shard_map.55) | data formatting | bytes 2097152

commit v4 on v3

--- a/solution.py
+++ b/solution.py
@@ -31,7 +31,7 @@
 def fused(
     plan, lengths_in, home_in, queries, keys, values, out,
     lengths, home, q, kv, qext, kext, mixed, give, keep, top, part_sum,
-    small_sem, load_sem, q_load, q_send, q_recv, kv_send, kv_recv, hop_send, hop_recv, o_send, o_recv, o_keep,
+    ready, small_sem, load_sem, q_load, q_send, q_recv, kv_send, kv_recv, hop_send, hop_recv, o_send, o_recv, o_keep,
 ):
     group, halves, depth, reach, windowed, chunk = plan
     rows = queries.shape[0]
@@ -136,15 +136,29 @@
     barrier = pltpu.get_barrier_semaphore()
     pl.semaphore_signal(barrier, inc=1, device_id={"seq": other}, device_id_type=MESH)
 
-    @pl.when(pair > 0)
+    @pl.when((parity == 0) & (pair > 0))
     def _():
         pl.semaphore_signal(barrier, inc=1, device_id={"seq": me - 2}, device_id_type=MESH)
 
-    pl.semaphore_wait(barrier, 1 + (pair < last).astype(jnp.int32))
+    @pl.when((parity == 1) & (pair < last))
+    def _():
+        pl.semaphore_signal(barrier, inc=1, device_id={"seq": me + 2}, device_id_type=MESH)
+
+    greeted = jnp.where(parity == 0, pair < last, pair > 0)
+    pl.semaphore_wait(barrier, 1 + greeted.astype(jnp.int32))
+
+    @pl.when((parity == 1) & (pair > 0))
+    def _():
+        pl.semaphore_signal(ready, inc=1, device_id={"seq": me - 2}, device_id_type=MESH)
 
     for h in range(halves):
         for t in range(2):
             swap_kv(h, t).start()
+
+    @pl.when((parity == 1) & (pair < last))
+    def _():
+        pl.semaphore_wait(ready, 1)
+
     for h in range(halves):
         for t in range(2):
             load_kv(h, t).wait()
@@ -411,6 +425,7 @@
             pltpu.VMEM((halves, group, rows, HD), bf16),
             pltpu.VMEM((group // plan[-1], blocks, plan[-1] * BLOCK, HD), jnp.float32),
             pltpu.VMEM((group // plan[-1], blocks, plan[-1] * BLOCK, 2 * HD), jnp.float32),
+            pltpu.SemaphoreType.REGULAR,
             dma((2,)),
             dma((halves, 2)),
             dma((halves, group)),

time: 35.1 us -> 34.5 us (0.983)
  the two profiles are of different devices: /device:TPU:0 before, /device:TPU:24 now
where the time goes in v4:
time: 34.5 us; the launch traced here: 34.3 us
  Pallas kernels  33.4 us (97%)
  local copies, waits for them, and re-layouts  0.97 us (3%)
    pallas_call x1, Pallas kernels, local(): pl.pallas_call(functools.partial(fused, plan), out_shape=pltpu.VMEM(queri...  33.4 us
    unnamed x1, local copies, waits for them, and re-layouts  0.97 us

profile of v4, /device:TPU:24, one launch (start us, length us, event | category | flops | bytes accessed | tf_op | source)
XLA Modules:
  0.0 34.3 jit_solution(7002662869092310505)
XLA Ops:
  0.0 33.4 %shard_map.55 = bf16[256,2048]{1,0:T(8,128)(2,1)S(1)} custom-call(s32[8]{0:T(128)} %lengths_in.1, s32[16]{0:T(128)} %home_in.1, bf16[256,2048]{1,0:T(8,128)(2,1)} %queries.1, bf16[256,512]{1,0:T(8,128)(2,1)} %keys.1, bf16[256,512]{1,0:T(8,128)(2,1)} %values.1), custom_call_target="tpu_custom_call" | custom-call | tf_op jit(solution)/shard_map/pallas_call | solution.py:411
  33.4 1.0 %copy.7 = bf16[256,2048]{1,0:T(8,128)(2,1)} copy(bf16[256,2048]{1,0:T(8,128)(2,1)S(1)} %shard_map.55) | data formatting | bytes 2097152

commit v5 on v4

--- a/solution.py
+++ b/solution.py
@@ -44,6 +44,8 @@
     pair = me // 2
     last = count // 2 - 1
     scale = HD ** (-0.5) * LOG2E
+    far = [j for j in range(blocks) if (depth, 0) in [run[:2] for run in spans(j, depth, blocks, reach)]]
+    split = depth > 0 and per > 1 and far == [0]
 
     def columns(head, wide=1):
         return pl.ds(pl.multiple_of(head * HD, HD), wide * HD)
@@ -82,43 +84,68 @@
             device_id_type=MESH,
         )
 
-    def hop(h, back, side):
+    def is_split(h, back, side):
+        return split and h == halves - 1 and back == depth - 1 and side == 0
+
+    def hop_rows(h, back, side, begin, end, part):
         return pltpu.make_async_remote_copy(
-            kv.at[h, :, back, side],
-            kv.at[h, :, back + 1, side],
-            hop_send.at[h, back, side],
-            hop_recv.at[h, back, side],
+            kv.at[h, :, back, side, pl.ds(begin, end - begin)],
+            kv.at[h, :, back + 1, side, pl.ds(begin, end - begin)],
+            hop_send.at[h, back, side, part],
+            hop_recv.at[h, back, side, part],
             device_id={"seq": me + 2},
             device_id_type=MESH,
         )
 
-    def send_out(h, g):
+    def last_hop():
+        return hop_rows(halves - 1, depth - 1, 0, 0, BLOCK, 1)
+
+    def each_hop(h, back, side, act):
+        if not (split and h == halves - 1 and back == depth - 1):
+            act(hop_rows(h, back, side, 0, rows, 0))
+            return
+        for fixed in range(2):
+
+            @pl.when(side == fixed)
+            def _():
+                act(hop_rows(h, back, fixed, BLOCK if is_split(h, back, fixed) else 0, rows, 0))
+
+    def out_part(h, g, slots):
+        at = pl.ds(slots[0] * BLOCK, len(slots) * BLOCK)
+        return at, out.at[at, columns((parity * halves + h) * group + g)]
+
+    def send_out(h, g, slots):
+        at, place = out_part(h, g, slots)
         return pltpu.make_async_remote_copy(
-            give.at[h, g],
-            out.at[:, columns((parity * halves + h) * group + g)],
-            o_send.at[h, g],
-            o_recv.at[h, g],
+            give.at[h, g, at],
+            place,
+            o_send.at[h, g, slots[0]],
+            o_recv.at[h, g, slots[0]],
             device_id={"seq": other},
             device_id_type=MESH,
         )
 
-    def keep_out(h, g):
-        return pltpu.make_async_copy(
-            keep.at[h, g], out.at[:, columns((parity * halves + h) * group + g)], o_keep.at[h, g]
-        )
+    def keep_out(h, g, slots):
+        at, place = out_part(h, g, slots)
+        return pltpu.make_async_copy(keep.at[h, g, at], place, o_keep.at[h, g, slots[0]])
+
+    def batches(h):
+        if split and h == halves - 1:
+            return [list(range(1, per)), [0]]
+        return [list(range(per))]
 
     def forward(h, back, side):
         if back > 0:
 
             @pl.when(pair >= back)
             def _():
-                hop(h, back - 1, side).wait_recv()
+                each_hop(h, back - 1, side, lambda copy: copy.wait_recv())
 
         if back < depth:
 
             @pl.when((pair >= back) & (pair < last))
             def _():
-                hop(h, back, side).start()
+                each_hop(h, back, side, lambda copy: copy.start())
 
     small = [
         pltpu.make_async_copy(lengths_in, lengths, small_sem.at[0]),
@@ -223,14 +250,17 @@
                 found.append(kv[h, t, back, side, at])
         return jnp.concatenate(found, axis=0)
 
-    def stages(j, own):
-        found = [[], [], []]
+    def stages(h, j, own):
+        found = [[], [], [], []]
         for back, low, high in spans(j, depth, blocks, reach):
             if back < depth or depth == 0:
                 found[0].append((back, low, high))
                 continue
             for stage, side in ((1, own), (2, 1 - own)):
                 begin, end = max(low, side * per), min(high, (side + 1) * per)
+                if begin < end and begin == 0 and is_split(h, back - 1, 0):
+                    found[3].append((back, 0, 1))
+                    begin = 1
                 if begin < end:
                     found[stage].append((back, begin, end))
         return found
@@ -294,7 +324,7 @@
 
     def attend(h, step, own, begin, end):
         for j in range(blocks):
-            found = stages(j, own)
+            found = stages(h, j, own)
             runs = sum(found[begin:end], [])
             if not runs:
                 continue
@@ -319,13 +349,14 @@
             def _():
                 attend(h, step, side, begin, end)
 
-    def deliver(h, first):
+    def deliver(h, first, slots):
         for g in range(chunk):
-            for s in range(per):
-                give[h, first + g, pl.ds(s * BLOCK, BLOCK)] = mixed[h, first + g, sent_at[s]]
-                keep[h, first + g, pl.ds(s * BLOCK, BLOCK)] = mixed[h, first + g, kept_at[s]]
-            send_out(h, first + g).start()
-            keep_out(h, first + g).start()
+            for s in slots:
+                at = pl.ds(s * BLOCK, BLOCK)
+                give[h, first + g, at] = mixed[h, first + g, sent_at[s]]
+                keep[h, first + g, at] = mixed[h, first + g, kept_at[s]]
+            send_out(h, first + g, slots).start()
+            keep_out(h, first + g, slots).start()
 
     def settle(h, step):
         for g in range(chunk):
@@ -350,6 +381,12 @@
         if h > 0:
             arrive(h, soon, sides[1:])
         arrive(h, later[:-1], sides)
+        if split and h == halves - 1:
+
+            @pl.when((pair >= depth - 1) & (pair < last))
+            def _():
+                last_hop().start()
+
         joined = 2 if h == 0 else 1
         if joined == 2:
             arrive(h, later[-1:], sides[:1])
@@ -364,17 +401,26 @@
 
         if joined == 1:
             arrive(h, later[-1:], sides[:1])
+        arrive(h, later[-1:], sides[1:])
+
+        @pl.loop(0, steps)
+        def _(step):
+            if joined == 1:
+                attend(h, step, 0, 1, 3)
+            else:
+                by_parity(h, step, 2, 3)
+            deliver(h, step * chunk, batches(h)[0])
+
+        if len(batches(h)) > 1:
+
+            @pl.when(pair >= depth)
+            def _():
+                last_hop().wait_recv()
 
             @pl.loop(0, steps)
             def _(step):
-                by_parity(h, step, 1, 2)
-
-        arrive(h, later[-1:], sides[1:])
-
-        @pl.loop(0, steps)
-        def _(step):
-            by_parity(h, step, 2, 3)
-            deliver(h, step * chunk)
+                attend(h, step, 0, 3, 4)
+                deliver(h, step * chunk, batches(h)[1])
 
     for h in range(halves):
         for t in range(2):
@@ -384,12 +430,19 @@
 
                 @pl.when((pair >= back) & (pair < last))
                 def _():
-                    hop(h, back, side).wait_send()
+                    each_hop(h, back, side, lambda copy: copy.wait_send())
 
         for g in range(group):
             swap_q(h, g).wait_send()
-            keep_out(h, g).wait()
-            send_out(h, g).wait()
+            for slots in batches(h):
+                keep_out(h, g, slots).wait()
+                send_out(h, g, slots).wait()
+
+    if split:
+
+        @pl.when((pair >= depth - 1) & (pair < last))
+        def _():
+            last_hop().wait_send()
 
 
 def local(queries, keys, values, lengths, home):
@@ -433,11 +486,11 @@
             dma((halves, group)),
             dma((halves, 2)),
             dma((halves, 2)),
-            dma((halves, depth, 2)),
-            dma((halves, depth, 2)),
-            dma((halves, group)),
-            dma((halves, group)),
-            dma((halves, group)),
+            dma((halves, depth, 2, 2)),
+            dma((halves, depth, 2, 2)),
+            dma((halves, group, rows // BLOCK)),
+            dma((halves, group, rows // BLOCK)),
+            dma((halves, group, rows // BLOCK)),
         ],
         compiler_params=pltpu.CompilerParams(
             collective_id=0, has_side_effects=True, vmem_limit_bytes=60 * 1024 * 1024

time: 34.5 us -> 34.2 us (level)
  Pallas kernels: 33.4 us -> 32.7 us
    pallas_call x1, Pallas kernels: 33.4 us -> 32.7 us  [local(): pl.pallas_call(functools.partial(fused, plan), out_shape=pltpu.VMEM(queri...]
where the time goes in v5:
time: 34.2 us; the launch traced here: 33.7 us
  Pallas kernels  32.7 us (96%)
  local copies, waits for them, and re-layouts  0.97 us (3%)
    pallas_call x1, Pallas kernels, local(): pl.pallas_call(functools.partial(fused, plan), out_shape=pltpu.VMEM(queri...  32.7 us
    unnamed x1, local copies, waits for them, and re-layouts  0.97 us

profile of v5, /device:TPU:24, one launch (start us, length us, event | category | flops | bytes accessed | tf_op | source)
XLA Modules:
  0.0 33.7 jit_solution(11621361629695119359)
XLA Ops:
  0.0 32.7 %shard_map.55 = bf16[256,2048]{1,0:T(8,128)(2,1)S(1)} custom-call(s32[8]{0:T(128)} %lengths_in.1, s32[16]{0:T(128)} %home_in.1, bf16[256,2048]{1,0:T(8,128)(2,1)} %queries.1, bf16[256,512]{1,0:T(8,128)(2,1)} %keys.1, bf16[256,512]{1,0:T(8,128)(2,1)} %values.1), custom_call_target="tpu_custom_call" | custom-call | tf_op jit(solution)/shard_map/pallas_call | solution.py:464
  32.8 1.0 %copy.7 = bf16[256,2048]{1,0:T(8,128)(2,1)} copy(bf16[256,2048]{1,0:T(8,128)(2,1)S(1)} %shard_map.55) | data formatting | bytes 2097152

commit v6 on v5

--- a/solution.py
+++ b/solution.py
@@ -93,7 +93,7 @@
             kv.at[h, :, back + 1, side, pl.ds(begin, end - begin)],
             hop_send.at[h, back, side, part],
             hop_recv.at[h, back, side, part],
-            device_id={"seq": me + 2},
+            device_id={"seq": (me + 2) % count},
             device_id_type=MESH,
         )
 

time: 34.2 us -> 34.2 us (level)
  no operation moved by 1% of the time
where the time goes in v6:
time: 34.2 us; the launch traced here: 33.7 us
  Pallas kernels  32.7 us (96%)
  local copies, waits for them, and re-layouts  0.97 us (3%)
    pallas_call x1, Pallas kernels, local(): pl.pallas_call(functools.partial(fused, plan), out_shape=pltpu.VMEM(queri...  32.7 us
    unnamed x1, local copies, waits for them, and re-layouts  0.97 us

profile of v6, /device:TPU:24, one launch (start us, length us, event | category | flops | bytes accessed | tf_op | source)
XLA Modules:
  0.0 33.7 jit_solution(4418542551989377708)
XLA Ops:
  0.0 32.7 %shard_map.55 = bf16[256,2048]{1,0:T(8,128)(2,1)S(1)} custom-call(s32[8]{0:T(128)} %lengths_in.1, s32[16]{0:T(128)} %home_in.1, bf16[256,2048]{1,0:T(8,128)(2,1)} %queries.1, bf16[256,512]{1,0:T(8,128)(2,1)} %keys.1, bf16[256,512]{1,0:T(8,128)(2,1)} %values.1), custom_call_target="tpu_custom_call" | custom-call | tf_op jit(solution)/shard_map/pallas_call | solution.py:464
  32.8 1.0 %copy.7 = bf16[256,2048]{1,0:T(8,128)(2,1)} copy(bf16[256,2048]{1,0:T(8,128)(2,1)S(1)} %shard_map.55) | data formatting | bytes 2097152
